TPU v7x, 512 devices: a whole 4x8x8 slice. The times are simulated.
512 devices in a mesh: tm: 16 (over x, z_hi, core), contact: 32 (over z_lo, y).
Axes of the slice: x: 4, y: 8, z: 8 (z_hi: 2, z_lo: 4; z = z_hi * 4 + z_lo), core: 2. Of those that a mesh axis runs over, the one named last changes fastest.
Arguments:
- signal: bfloat16 [8, 512, 16384], P(None, 'contact', 'tm'), may hold values from -6 to 6
- fir_taps: bfloat16 [512, 129], P('contact'), may hold values from -0.5 to 0.5
- neighbours: int32 [512, 4], replicated, may hold values from 0 to 511, as said below
- live_mask: int32 [512], replicated, may hold values 0 or 1
- lap_coef: float32 [512], replicated, may hold values from 0.1 to 1
- w_query: bfloat16 [256, 256], replicated, may hold values from -8 to 8
- w_key: bfloat16 [256, 256], replicated, may hold values from -8 to 8
- w_value: bfloat16 [256, 256], replicated, may hold values from -0.375 to 0.375
- w_out: bfloat16 [256, 256], replicated, may hold values from -0.375 to 0.375
- cotangent: bfloat16 [8, 512, 16384], P(None, 'contact', 'tm'), may hold values from -6 to 6
Outputs:
- attended: bfloat16 [8, 512, 16384], P(None, 'contact', 'tm')
- weight_grads: float32 [4, 256, 256], replicated
Inputs may be any that keep to these rules, and one draw needn't show every extreme that they name: `neighbours`: entry [c, k] names a contact whose grid row (index // 16) differs from that of contact c by at most one and whose column (index % 16) differs by at most two.
All inputs are finite; a program needn't handle non-finite values.
Results may differ from a plain program's by a relative error of at most 0.011.
Values may be sent and summed in bfloat16 or wider, within the bound.
A program may use at most 64 MiB of HBM per device.

v0:
```python
import jax
import jax.numpy as jnp
from jax import lax
from jax.sharding import PartitionSpec as P

GRID_COLS = 16
HEADS = 4


def from_behind(value, axis, by):
    count = lax.axis_size(axis)
    pairs = [(i, i + by) for i in range(count) if 0 <= i + by < count]
    return lax.ppermute(value, axis, pairs)


def extended_2(cells, sides, width):
    for axis, dim in sides:
        count = lax.axis_size(axis)
        ends = count - 1
        head = lax.slice_in_dim(cells, 0, width, axis=dim)
        tail = lax.slice_in_dim(cells, cells.shape[dim] - width, cells.shape[dim], axis=dim)
        cells = jnp.concatenate(
            [
                lax.ppermute(tail, axis, [(i, (i + 1) % count) for i in range(ends)]),
                cells,
                lax.ppermute(head, axis, [((i + 1) % count, i) for i in range(ends)]),
            ],
            axis=dim,
        )
    return cells


def contract(left, right, left_dim, right_dim):
    return lax.dot_general(
        left, right, (((left_dim,), (right_dim,)), ((), ())), preferred_element_type=jnp.float32
    )


def toeplitz(fir_taps):
    rim_width = fir_taps.shape[1] - 1
    source = jnp.arange(2 * rim_width, dtype=jnp.int32)[:, None]
    target = jnp.arange(rim_width, dtype=jnp.int32)[None, :]
    lag_table = target + rim_width - source
    inside = (lag_table >= 0) & (lag_table <= rim_width)
    picked = jnp.take(fir_taps, jnp.clip(lag_table, 0, rim_width), axis=1)
    return jnp.where(inside[None, :, :], picked, jnp.zeros_like(picked))


def laplace(field, centre, indices, nbr_alive, own_alive, coef):
    source_ids = jnp.arange(field.shape[-2], dtype=jnp.int32)
    counts = jnp.zeros((indices.shape[0], field.shape[-2]), jnp.float32)
    for slot_index in range(indices.shape[1]):
        hit = (indices[:, slot_index][:, None] == source_ids[None, :]).astype(jnp.float32)
        counts = counts + nbr_alive[:, slot_index][:, None] * hit
    alive_count = jnp.sum(nbr_alive, axis=1)
    beside = jnp.einsum(
        "cn,bnt->bct", counts.astype(jnp.bfloat16), field, preferred_element_type=jnp.float32
    )
    middle = centre.astype(jnp.float32)
    running = beside - alive_count[:, None] * middle
    return (own_alive[:, None] * (middle + coef[:, None] * running)).astype(jnp.bfloat16)


def one_head(query_head, key_head, value_head, back_head, key_alive, score_scale):
    scores = contract(query_head, key_head, 1, 1) * score_scale
    scores = jnp.where(key_alive[None, :] > 0, scores, -1e30)
    top_score = jnp.max(scores, axis=1, keepdims=True)
    raised = jnp.exp(scores - top_score)
    attn_prob = raised / jnp.sum(raised, axis=1, keepdims=True)
    prob_low = attn_prob.astype(jnp.bfloat16)
    head_out = jnp.dot(prob_low, value_head, preferred_element_type=jnp.float32).astype(
        jnp.bfloat16
    )
    grad_value = contract(prob_low, back_head, 0, 0).astype(jnp.bfloat16)
    grad_prob = contract(back_head, value_head, 1, 1)
    row_inner = jnp.sum(
        back_head.astype(jnp.float32) * head_out.astype(jnp.float32), axis=1, keepdims=True
    )
    grad_score = (attn_prob * (grad_prob - row_inner) * score_scale).astype(jnp.bfloat16)
    grad_query = jnp.dot(grad_score, key_head, preferred_element_type=jnp.float32).astype(
        jnp.bfloat16
    )
    grad_key = contract(grad_score, query_head, 0, 0).astype(jnp.bfloat16)
    return (head_out, grad_query, grad_key, grad_value)


def group_step(tokens, upstream, key_alive, w_query, w_key, w_value, w_out):
    as_float = tokens.astype(jnp.float32)
    normed = (
        as_float * lax.rsqrt(jnp.mean(as_float * as_float, axis=1, keepdims=True) + 1e-05)
    ).astype(jnp.bfloat16)
    query_rows = jnp.dot(normed, w_query, preferred_element_type=jnp.float32).astype(jnp.bfloat16)
    key_rows = jnp.dot(normed, w_key, preferred_element_type=jnp.float32).astype(jnp.bfloat16)
    value_rows = jnp.dot(normed, w_value, preferred_element_type=jnp.float32).astype(jnp.bfloat16)
    back_signal = contract(upstream, w_out, 1, 1).astype(jnp.bfloat16)
    head_size = w_query.shape[1] // HEADS
    score_scale = head_size ** (-0.5)
    head_results = []
    for head_index in range(HEADS):
        lower = head_index * head_size
        upper = lower + head_size
        head_results.append(
            one_head(
                query_rows[:, lower:upper],
                key_rows[:, lower:upper],
                value_rows[:, lower:upper],
                back_signal[:, lower:upper],
                key_alive,
                score_scale,
            )
        )
    mixed_heads = jnp.concatenate([entry[0] for entry in head_results], axis=1)
    grad_query = jnp.concatenate([entry[1] for entry in head_results], axis=1)
    grad_key = jnp.concatenate([entry[2] for entry in head_results], axis=1)
    grad_value = jnp.concatenate([entry[3] for entry in head_results], axis=1)
    attended = jnp.dot(mixed_heads, w_out, preferred_element_type=jnp.float32).astype(jnp.bfloat16)
    grad_stack = jnp.stack(
        [
            contract(normed, grad_query, 0, 0),
            contract(normed, grad_key, 0, 0),
            contract(normed, grad_value, 0, 0),
            contract(mixed_heads, upstream, 0, 0),
        ]
    )
    return (attended, grad_stack)


def to_groups(whole, patch_len):
    batch_size, contacts_here, slab_len = whole.shape
    patch_count = slab_len // patch_len
    shaped = whole.reshape(batch_size, contacts_here, patch_count, patch_len).transpose(0, 2, 1, 3)
    return shaped.reshape(batch_size * patch_count, contacts_here, patch_len)


def from_groups(grouped, batch_size):
    group_count, contacts_here, patch_len = grouped.shape
    patch_count = group_count // batch_size
    shaped = grouped.reshape(batch_size, patch_count, contacts_here, patch_len).transpose(
        0, 2, 1, 3
    )
    return shaped.reshape(batch_size, contacts_here, patch_count * patch_len)


def local(
    signal, fir_taps, neighbours, live_mask, lap_coef, w_query, w_key, w_value, w_out, cotangent
):
    batch_size, contacts_here, slab_len = signal.shape
    rim_width = fir_taps.shape[1] - 1
    patch_len = w_query.shape[0]
    patch_count = slab_len // patch_len
    prior_rim = from_behind(signal[:, :, slab_len - rim_width :], "tm", 1)
    extended = jnp.concatenate([prior_rim, signal], axis=2)
    blocks = extended.reshape(batch_size, contacts_here, slab_len // rim_width + 1, rim_width)
    windows = jnp.concatenate([blocks[:, :, :-1], blocks[:, :, 1:]], axis=3)
    filter_table = toeplitz(fir_taps)
    filtered = jnp.einsum(
        "bcjw,cwu->bcju", windows, filter_table, preferred_element_type=jnp.float32
    )
    filtered = filtered.reshape(batch_size, contacts_here, slab_len).astype(jnp.bfloat16)
    alive_f = live_mask.astype(jnp.float32)
    nbr_alive = jnp.take(alive_f, neighbours)
    first_contact = lax.axis_index("contact") * contacts_here
    padded = extended_2(filtered, (("contact", 1),), GRID_COLS)
    local_index = (
        lax.dynamic_slice_in_dim(neighbours, first_contact, contacts_here, 0)
        - first_contact
        + GRID_COLS
    )
    ready = laplace(
        padded,
        filtered,
        local_index,
        lax.dynamic_slice_in_dim(nbr_alive, first_contact, contacts_here, 0),
        lax.dynamic_slice_in_dim(alive_f, first_contact, contacts_here, 0),
        lax.dynamic_slice_in_dim(lap_coef, first_contact, contacts_here, 0),
    )
    grouped = to_groups(ready, patch_len)
    features, upstream = (
        lax.all_to_all(grouped, "contact", split_axis=0, concat_axis=1, tiled=True),
        lax.all_to_all(
            to_groups(cotangent, patch_len), "contact", split_axis=0, concat_axis=1, tiled=True
        ),
    )

    def run_group(running, inputs_pair):
        attended, grad_stack = group_step(
            inputs_pair[0], inputs_pair[1], alive_f, w_query, w_key, w_value, w_out
        )
        return (running + grad_stack, attended)

    running, attended_groups = lax.scan(
        run_group, jnp.zeros((4, patch_len, patch_len), jnp.float32), (features, upstream)
    )
    summed = lax.psum(running, ("tm", "contact"))
    returned = lax.all_to_all(attended_groups, "contact", split_axis=1, concat_axis=0, tiled=True)
    attended = from_groups(returned, batch_size)
    grad_scale = (batch_size * patch_count * lax.axis_size("tm") * neighbours.shape[0]) ** (-0.5)
    return (attended, summed * grad_scale)


def solution(mesh):
    in_specs = (
        P(None, "contact", "tm"),
        P("contact", None),
        P(),
        P(),
        P(),
        P(),
        P(),
        P(),
        P(),
        P(None, "contact", "tm"),
    )
    out_specs = (P(None, "contact", "tm"), P())
    return jax.shard_map(local, mesh=mesh, in_specs=in_specs, out_specs=out_specs, check_vma=False)
```

profile of v0, /device:TPU:1, one launch (start us, length us, event | category | flops | bytes accessed | tf_op | source)
XLA Modules:
  0.0 490.4 jit_solution(11078941743470237049)
XLA Ops:
  7.2 0.8 slice.121
  8.0 12.0 %collective-permute-start = (bf16[8,16,128]{2,1,0:T(8,128)(2,1)S(1)}, bf16[8,16,128]{2,1,0:T(8,128)(2,1)S(1)}, u32[]{:S(2)}, u32[]{:S(2)}) collective-permute-start(bf16[8,16,128]{2,1,0:T(8,128)(2,1)S(1)} %slice.121), channel_id=1, source_target_pairs={{0,32},{32,64},{64,96},{96,128},{128,160},{160,192},{192,224},{224... | collective-permute-start | bytes 98312 | tf_op jit(solution)/shard_map/ppermute | solution.py:13
  20.0 1.0 fusion.132
  21.0 0.7 pad_maximum_fusion.5
  21.7 9.9 %all-to-all-start.2 = ((bf16[32,16,256]{2,1,0:T(8,128)(2,1)}), bf16[32,16,256]{2,1,0:T(8,128)(2,1)S(1)}, u32[]{:S(2)}, u32[]{:S(2)}) async-start(bf16[32,16,256]{2,1,0:T(8,128)(2,1)} %bitcast.20), calls=%async_computation.2 | async-start | bytes 524288 | tf_op jit(solution)/shard_map/all_to_all | solution.py:180
  32.2 13.2 %gather_fusion.1 = f32[2048]{0:T(1024)S(1)} fusion(f32[512]{0:T(512)S(1)} %convert_element_type.188, s32[2048]{0:T(1024)S(1)} %broadcast_clamp_fusion), kind=kCustom, calls=%fused_computation.1 | custom fusion | bytes 24576 | tf_op jit(solution)/shard_map/jit(_take)/gather | solution.py:161
  45.4 0.3 reshape.181
  46.0 114.2 %gather_fusion = bf16[32768,16]{1,0:T(8,128)(2,1)} fusion(bf16[16,129]{0,1:T(8,128)(2,1)S(1)} %copy.116, s32[32768]{0:T(1024)S(1)} %fusion.71), kind=kCustom, calls=%fused_computation | custom fusion | bytes 2228224 | tf_op jit(solution)/shard_map/jit(_take)/gather | solution.py:45
  160.2 6.9 %copy.117 = bf16[256,128,16]{1,0,2:T(8,128)(2,1)S(1)} copy(bf16[256,128,16]{2,1,0:T(8,128)(2,1)} %bitcast.104) | data formatting | bytes 2097152 | tf_op jit(solution)/shard_map/jit(_take)/gather | solution.py:45
  167.4 0.4 fusion.22
  168.1 1.3 collective-permute-start.2
  169.4 4.0 collective-permute-start.1
  173.6 0.8 dynamic_slice.18
  174.3 0.9 collective-permute-done.2
  175.2 1.5 collective-permute-done.1
  176.7 0.3 fusion.20
  177.1 0.7 pad_maximum_fusion.3
  177.8 11.5 %all-to-all-start = ((bf16[32,16,256]{2,1,0:T(8,128)(2,1)}), bf16[32,16,256]{2,1,0:T(8,128)(2,1)S(1)}, u32[]{:S(2)}, u32[]{:S(2)}) async-start(bf16[32,16,256]{2,1,0:T(8,128)(2,1)} %bitcast.16), calls=%async_computation | async-start | bytes 524288 | tf_op jit(solution)/shard_map/all_to_all | solution.py:179
  189.3 0.2 all-reduce.2.cloned.1.call-start
  189.6 0.3 convolution_convert_fusion
  189.9 9.5 %all-to-all-done = bf16[32,16,256]{2,1,0:T(8,128)(2,1)S(1)} async-done(((bf16[32,16,256]{2,1,0:T(8,128)(2,1)}), bf16[32,16,256]{2,1,0:T(8,128)(2,1)S(1)}, u32[]{:S(2)}, u32[]{:S(2)}) %all-to-all-start) | async-done | bytes 262176 | tf_op jit(solution)/shard_map/all_to_all | solution.py:179
  199.8 0.3 convolution_convert_fusion.3
  200.1 0.3 convolution_convert_fusion.4
  200.4 0.4 fusion.134
  200.7 0.4 fusion.135
  201.1 0.4 fusion.136
  201.5 0.4 fusion.137
  202.2 0.5 copy-done.4
  202.7 0.3 convolution_convert_fusion.2
  203.0 0.2 fusion.33
  203.4 0.2 convolution_convert_fusion.10
  203.6 0.2 convolution_convert_fusion.11
  203.8 0.3 convolution_convert_fusion.14
  204.1 0.3 convolution_convert_fusion.15
  204.7 0.2 convolution_convert_fusion.12
  205.0 0.3 convolution_convert_fusion.16
  205.6 0.3 convolution_convert_fusion.17
  205.9 0.2 multiply_reduce_fusion.4
  206.1 0.4 fusion.12
  206.5 0.3 convolution_convert_fusion.18
  206.8 0.2 convolution_convert_fusion.6
  207.0 0.4 fusion.13
  207.4 0.3 convolution_convert_fusion.19
  207.7 0.2 convolution_convert_fusion.7
  207.9 0.4 fusion.14
  208.3 0.3 convolution_convert_fusion.20
  208.6 0.2 convolution_convert_fusion.8
  208.8 0.4 fusion.15
  209.2 0.3 convolution_convert_fusion.21
  209.5 0.2 convolution_convert_fusion.9
  209.7 0.2 convolution_bitcast_fusion.1
  210.0 0.3 convolution_bitcast_fusion.2
  210.2 0.3 convolution_bitcast_fusion.3
  210.5 0.3 convolution_bitcast_fusion.4
  210.8 1.0 pad_maximum_fusion
  211.9 0.3 fusion.21
  212.1 0.4 copy.146
  212.6 0.5 broadcast.198
  213.1 2.2 reduce.4
  215.4 14.6 %all_to_all.12 = bf16[32,2,2048]{2,1,0:T(2,128)(2,1)S(1)} all-to-all(bf16[32,2,2048]{2,1,0:T(2,128)(2,1)S(1)} %reshape.193), channel_id=1, replica_groups=mesh['tm'=16,'contact'=32] {'contact'}, dimensions={0} | all-to-all | bytes 524288 | tf_op jit(solution)/shard_map/all_to_all | solution.py:195
  230.0 0.3 reshape.194
  230.3 0.7 copy.142
  231.1 250.2 %all-reduce.2.cloned.1.call-done = f32[4,256,256]{2,1,0:T(8,128)} async-done(((f32[4,256,256]{2,1,0:T(8,128)}), f32[4,256,256]{2,1,0:T(8,128)}) %all-reduce.2.cloned.1.call-update) | async-done | bytes 1048592 | tf_op jit(solution)/shard_map/psum | solution.py:194
  481.3 2.3 broadcast_multiply_fusion
  (54 shorter events, 3.4 us)
Async XLA Ops:
  7.2 182.4 %copy-start = (bf16[256,256]{1,0:T(8,128)(2,1)S(1)}, bf16[256,256]{1,0:T(8,128)(2,1)}, u32[]{:S(2)}) copy-start(bf16[256,256]{1,0:T(8,128)(2,1)} %param.18) | copy-start | bytes 393220
  7.2 24.7 %copy-start.6 = (s32[512]{0:T(512)S(1)}, s32[512]{0:T(512)}, u32[]{:S(2)}) copy-start(s32[512]{0:T(512)} %param.13) | copy-start | bytes 6148
  7.2 24.7 %copy-start.5 = (s32[512,4]{0,1:T(4,128)S(1)}, s32[512,4]{0,1:T(4,128)}, u32[]{:S(2)}) copy-start(s32[512,4]{0,1:T(4,128)} %param.12) | copy-start | bytes 24580
  8.0 159.1 %collective-permute-start = (bf16[8,16,128]{2,1,0:T(8,128)(2,1)S(1)}, bf16[8,16,128]{2,1,0:T(8,128)(2,1)S(1)}, u32[]{:S(2)}, u32[]{:S(2)}) collective-permute-start(bf16[8,16,128]{2,1,0:T(8,128)(2,1)S(1)} %slice.121), channel_id=1, source_target_pairs={{0,32},{32,64},{64,96},{96,128},{128,160},{160,192},{192,224},{224... | collective-permute-start | bytes 98312 | tf_op jit(solution)/shard_map/ppermute | solution.py:13
  21.7 156.1 %all-to-all-start.2 = ((bf16[32,16,256]{2,1,0:T(8,128)(2,1)}), bf16[32,16,256]{2,1,0:T(8,128)(2,1)S(1)}, u32[]{:S(2)}, u32[]{:S(2)}) async-start(bf16[32,16,256]{2,1,0:T(8,128)(2,1)} %bitcast.20), calls=%async_computation.2 | async-start | bytes 524288 | tf_op jit(solution)/shard_map/all_to_all | solution.py:180
  32.2 13.7 %copy-start.7 = (bf16[16,129]{1,0:T(8,128)(2,1)S(1)}, bf16[16,129]{1,0:T(8,128)(2,1)}, u32[]{:S(2)}) copy-start(bf16[16,129]{1,0:T(8,128)(2,1)} %param.11) | copy-start | bytes 12388
  160.2 6.9 %copy-start.1 = (bf16[8,16,1024]{2,1,0:T(8,128)(2,1)S(1)}, bf16[8,16,1024]{2,1,0:T(8,128)(2,1)}, u32[]{:S(2)}) copy-start(bf16[8,16,1024]{2,1,0:T(8,128)(2,1)} %param.10) | copy-start | bytes 786436
  168.1 7.1 %collective-permute-start.2 = (bf16[8,16,1024]{2,1,0:T(8,128)(2,1)S(1)}, bf16[8,16,1024]{2,1,0:T(8,128)(2,1)S(1)}, u32[]{:S(2)}, u32[]{:S(2)}) collective-permute-start(bf16[8,16,1024]{2,1,0:T(8,128)(2,1)S(1)} %copy.120), channel_id=1, source_target_pairs={{1,0},{2,1},{3,2},{4,3},{5,4},{6,5},{7,6},{8,7},{9,8},{10,9},{11,1... | collective-permute-start | bytes 786440 | tf_op jit(solution)/shard_map/ppermute | solution.py:26
  169.4 7.3 %collective-permute-start.1 = (bf16[8,16,1024]{2,1,0:T(8,128)(2,1)S(1)}, bf16[8,16,1024]{2,1,0:T(8,128)(2,1)S(1)}, u32[]{:S(2)}, u32[]{:S(2)}) collective-permute-start(bf16[8,16,1024]{2,1,0:T(8,128)(2,1)S(1)} %copy.120), channel_id=1, source_target_pairs={{0,1},{1,2},{2,3},{3,4},{4,5},{5,6},{6,7},{7,8},{8,9},{9,10},{10,1... | collective-permute-start | bytes 786440 | tf_op jit(solution)/shard_map/ppermute | solution.py:24
  177.0 22.7 %copy-start.2 = (bf16[256,256]{1,0:T(8,128)(2,1)S(1)}, bf16[256,256]{1,0:T(8,128)(2,1)}, u32[]{:S(2)}) copy-start(bf16[256,256]{1,0:T(8,128)(2,1)} %param.16) | copy-start | bytes 393220
  177.1 23.0 %copy-start.3 = (bf16[256,256]{1,0:T(8,128)(2,1)S(1)}, bf16[256,256]{1,0:T(8,128)(2,1)}, u32[]{:S(2)}) copy-start(bf16[256,256]{1,0:T(8,128)(2,1)} %param.15) | copy-start | bytes 393220
  177.8 21.6 %all-to-all-start = ((bf16[32,16,256]{2,1,0:T(8,128)(2,1)}), bf16[32,16,256]{2,1,0:T(8,128)(2,1)S(1)}, u32[]{:S(2)}, u32[]{:S(2)}) async-start(bf16[32,16,256]{2,1,0:T(8,128)(2,1)} %bitcast.16), calls=%async_computation | async-start | bytes 524288 | tf_op jit(solution)/shard_map/all_to_all | solution.py:179
  189.3 291.9 %all-reduce.2.cloned.1.call-start = ((), (), s32[]{:S(2)}) async-start(), calls=%async_computation.3 | async-start | bytes 2097152 | tf_op jit(solution)/shard_map/psum | solution.py:194
  201.8 0.9 copy-start.4
Sparse Core Ops, SparseCore 0:
  212.0 269.2 all-reduce.1
where the time goes:
time: 491 us; the launch traced here: 490 us
  waiting for transfers between devices  262 us (53%)
  local copies, waits for them, and re-layouts  141 us (29%)
  starting transfers between devices  39 us (8%)
  blocking collectives  14.6 us (3%)
  between operations  14.6 us (3%)
  matrix products  10.1 us (2%)
  other arithmetic  9.12 us (2%)
    psum x1, waiting for transfers between devices, local(): summed = lax.psum(running, ('tm', 'contact'))  250 us
    gather x2, local copies, waits for them, and re-layouts, toeplitz(): picked = jnp.take(fir_taps, jnp.clip(lag_table, 0, rim_width), axis=1)  121 us
    all_to_all x1, blocking collectives, local(): lax.all_to_all(attended_groups, 'contact', split_axis=1, concat_axis=0, t...  14.6 us
    gather x2, local copies, waits for them, and re-layouts, local(): nbr_alive = jnp.take(alive_f, neighbours)  13.5 us
    ppermute x1, starting transfers between devices, from_behind(): return lax.ppermute(value, axis, pairs)  12 us
    all_to_all x1, starting transfers between devices, local(): lax.all_to_all(grouped, 'contact', split_axis=0, concat_axis=1, tiled=True)  11.5 us
    all_to_all x1, starting transfers between devices, local(): lax.all_to_all(to_groups(cotangent, patch_len), 'contact', split_axis=0,...  9.94 us
  transfers between devices with their start and end apart: 6, of which 4 were waited for; matrix products, arithmetic and copies ran while one was open for 30% of the time, Pallas kernels for 0%

commit v1 on v0

v1 whole, which is shorter than its diff:
```python
import functools

import jax
import jax.numpy as jnp
from jax import lax
from jax.experimental import pallas as pl
from jax.experimental.pallas import tpu as pltpu
from jax.sharding import PartitionSpec as P

HEADS = 4
CORES = 2
HALVES = 2
SIDE_LAYERS = 4
MESH = pl.DeviceIdType.MESH
F32 = jnp.float32
BF16 = jnp.bfloat16


def nn(left, right):
    return lax.dot_general(left, right, (((1,), (0,)), ((), ())), preferred_element_type=F32)


def nt(left, right):
    return lax.dot_general(left, right, (((1,), (1,)), ((), ())), preferred_element_type=F32)


def build_tables(taps_ref, table_ref):
    contacts, taps = taps_ref.shape
    width = taps - 1
    values = taps_ref[...].astype(F32)
    source = lax.broadcasted_iota(jnp.int32, (width, width), 0)
    target = lax.broadcasted_iota(jnp.int32, (width, width), 1)
    for c in range(contacts):
        row = jnp.broadcast_to(values[c : c + 1, :width], (width, width))
        turned = pltpu.roll(row, 0, 1, stride=1, stride_axis=0)
        last = jnp.broadcast_to(values[c : c + 1, width:], (width, width))
        own = jnp.where(target >= source, turned, 0.0)
        before = jnp.where(target < source, turned, jnp.where(target == source, last, 0.0))
        table_ref[c, :, :width] = before.astype(BF16)
        table_ref[c, :, width:] = own.astype(BF16)


def spread_blocks(signal_ref, rows_ref, width):
    batch, contacts, length = signal_ref.shape
    blocks = length // width
    for b in range(batch):
        for j in range(blocks):
            at = (b * blocks + j) * contacts
            rows_ref[at : at + contacts, :] = signal_ref[
                b, :, j * width : (j + 1) * width
            ].astype(F32)


def run_filter(rows_ref, table_ref, before_ref, own_ref, filtered_ref):
    batch, contacts, length = filtered_ref.shape
    width = table_ref.shape[1]
    blocks = length // width
    count = batch * blocks
    for c in range(contacts):
        picked = rows_ref[pl.ds(c, count, stride=contacts), :].astype(BF16)
        both = nn(picked, table_ref[c])
        before_ref[pl.ds(c, count, stride=contacts), :] = both[:, :width]
        own_ref[pl.ds(c, count, stride=contacts), :] = both[:, width:]
    for b in range(batch):
        for j in range(1, blocks):
            at = (b * blocks + j) * contacts
            filtered_ref[b, :, j * width : (j + 1) * width] = (
                before_ref[at - contacts : at, :] + own_ref[at : at + contacts, :]
            ).astype(BF16)


def finish_filter(halo_ref, rows_ref, table_ref, before_ref, own_ref, filtered_ref):
    batch, contacts, length = filtered_ref.shape
    width = table_ref.shape[1]
    blocks = length // width
    for b in range(batch):
        rows_ref[b * contacts : (b + 1) * contacts, :] = halo_ref[b].astype(F32)
    for c in range(contacts):
        picked = rows_ref[pl.ds(c, batch, stride=contacts), :].astype(BF16)
        before_ref[pl.ds(c, batch, stride=contacts), :] = nn(picked, table_ref[c, :, :width])
    for b in range(batch):
        at = b * blocks * contacts
        filtered_ref[b, :, :width] = (
            before_ref[b * contacts : (b + 1) * contacts, :] + own_ref[at : at + contacts, :]
        ).astype(BF16)


def count_hits(neighbours_ref, alive_ref, coef_ref, hits_ref, columns_ref):
    slots, tokens = neighbours_ref.shape
    alive_row = alive_ref[...].astype(F32)
    stacked = jnp.concatenate(
        [neighbours_ref[...].astype(F32), alive_row, coef_ref[...]]
        + [jnp.zeros((8 - slots - 2, tokens), F32)],
        axis=0,
    )
    columns = stacked.T
    step = 128
    for at in range(0, tokens, step):
        ids = lax.broadcasted_iota(jnp.int32, (step, tokens), 1).astype(F32)
        hits = jnp.zeros((step, tokens), F32)
        for k in range(slots):
            hits = hits + jnp.where(columns[at : at + step, k : k + 1] == ids, alive_row, 0.0)
        hits_ref[at : at + step, :] = hits.astype(BF16)
        total = jnp.sum(hits, axis=1, keepdims=True)
        columns_ref[0, at : at + step, :] = jnp.broadcast_to(total, (step, 128))
    alive = columns[:, slots : slots + 1]
    columns_ref[1] = jnp.broadcast_to(alive, (tokens, 128))
    columns_ref[2] = jnp.broadcast_to(columns[:, slots + 1 : slots + 2], (tokens, 128))
    columns_ref[3] = jnp.broadcast_to(jnp.where(alive > 0, 0.0, -1e30), (tokens, 128))


def wide(column, lanes):
    return jnp.concatenate([column] * (lanes // column.shape[1]), axis=1)


def project_tokens(tokens_ref, hits_ref, columns_ref, weights, work):
    w_query_ref, w_key_ref, w_value_ref, _ = weights
    tokens, patch = tokens_ref.shape
    middle = tokens_ref[...]
    beside = nn(hits_ref[...], middle)
    middle = middle.astype(F32)
    alive_count, alive, coef = [wide(columns_ref[k], patch) for k in range(3)]
    ready = (alive * (middle + coef * (beside - alive_count * middle))).astype(BF16).astype(F32)
    mean = jnp.sum(ready * ready, axis=1, keepdims=True) * (1.0 / patch)
    normed_f = ready * lax.rsqrt(mean + 1e-05)
    normed = normed_f.astype(BF16)
    work["normed_t"][...] = normed_f.T.astype(BF16)
    score_scale = (patch // HEADS) ** (-0.5)
    query = nn(normed, w_query_ref[...]).astype(BF16).astype(F32)
    work["query"][...] = (query * score_scale).astype(BF16)
    keys = nn(normed, w_key_ref[...]).astype(BF16)
    work["key"][...] = keys
    work["key_t"][...] = keys.astype(F32).T.astype(BF16)
    values = nn(normed, w_value_ref[...]).astype(BF16)
    work["value"][...] = values
    work["value_t"][...] = values.astype(F32).T.astype(BF16)


def attend(upstream_ref, columns_ref, weights, work):
    w_out_ref = weights[3]
    tokens, patch = upstream_ref.shape
    head = patch // HEADS
    score_scale = head ** (-0.5)
    back = nt(upstream_ref[...], w_out_ref[...]).astype(BF16)
    work["back"][...] = back
    work["back_t"][...] = back.astype(F32).T
    pair = 2 * head
    lane = lax.broadcasted_iota(jnp.int32, (tokens, pair), 1)
    bias = wide(columns_ref[3], tokens)
    for p in range(HEADS // 2):
        at = slice(p * pair, (p + 1) * pair)
        grad_key = None
        grad_value = None
        for s in range(2):
            h = 2 * p + s
            rows = slice(h * head, (h + 1) * head)
            inside = (lane >= s * head) & (lane < (s + 1) * head)
            query = jnp.where(inside, work["query"][:, at].astype(F32), 0.0).astype(BF16)
            backward = jnp.where(inside, work["back"][:, at].astype(F32), 0.0).astype(BF16)
            scores = nt(work["key"][:, at], query) + bias
            raised = jnp.exp(scores - jnp.max(scores, axis=0, keepdims=True))
            prob = raised * (1.0 / jnp.sum(raised, axis=0, keepdims=True))
            prob_low = prob.astype(BF16)
            mixed_t = nn(work["value_t"][rows, :], prob_low).astype(BF16)
            work["mixed_t"][rows, :] = mixed_t
            inner = jnp.sum(
                work["back_t"][rows, :] * mixed_t.astype(F32), axis=0, keepdims=True
            )
            grad_prob = nt(work["value"][:, at], backward)
            grad_score = (prob * (grad_prob - inner)).astype(BF16)
            part_value = nn(prob_low, backward)
            part_key = nn(grad_score, query)
            grad_value = part_value if s == 0 else grad_value + part_value
            grad_key = part_key if s == 0 else grad_key + part_key
            work["grad_query_t"][rows, :] = (
                nn(work["key_t"][rows, :], grad_score) * score_scale
            ).astype(BF16)
        work["grad_key"][:, at] = grad_key.astype(BF16)
        work["grad_value"][:, at] = grad_value.astype(BF16)


def weight_grads(grads_ref, upstream_ref, work, grad_scale):
    patch = upstream_ref.shape[1]
    normed_t = work["normed_t"][...]
    products = (
        nt(normed_t, work["grad_query_t"][...]),
        nn(normed_t, work["grad_key"][...]),
        nn(normed_t, work["grad_value"][...]),
        nn(work["mixed_t"][...], upstream_ref[...]),
    )
    for k, product in enumerate(products):
        grads_ref[k * patch : (k + 1) * patch, :] = product * grad_scale


WORK = (
    ("query", 0, BF16),
    ("key", 0, BF16),
    ("value", 0, BF16),
    ("back", 0, BF16),
    ("grad_key", 0, BF16),
    ("grad_value", 0, BF16),
    ("key_t", 1, BF16),
    ("value_t", 1, BF16),
    ("back_t", 1, F32),
    ("normed_t", 1, BF16),
    ("mixed_t", 1, BF16),
    ("grad_query_t", 1, BF16),
)


def step_kernel(
    slabs,
    members,
    grad_scale,
    signal_ref,
    taps_ref,
    neighbours_ref,
    alive_ref,
    coef_ref,
    w_query_ref,
    w_key_ref,
    w_value_ref,
    w_out_ref,
    cotangent_ref,
    returned_ref,
    summed_ref,
    halo_ref,
    table_ref,
    rows_ref,
    before_ref,
    own_ref,
    filtered_ref,
    tokens_ref,
    upstream_ref,
    attended_ref,
    hits_ref,
    columns_ref,
    grads_ref,
    core_out,
    core_in,
    plane_sum,
    plane_out,
    plane_in,
    depth_in,
    result,
    send_sem,
    recv_sem,
    local_sem,
    *work_refs,
):
    work = {entry[0]: ref for entry, ref in zip(WORK, work_refs)}
    weights = (w_query_ref, w_key_ref, w_value_ref, w_out_ref)
    slab = lax.axis_index("tm")
    me = lax.axis_index("contact")
    core = lax.rem(slab, CORES)
    side = lax.rem(slab // CORES, HALVES)
    column = slab // (CORES * HALVES)
    columns = slabs // (CORES * HALVES)
    layers = SIDE_LAYERS
    lines = members // layers
    layer = me // lines
    line = lax.rem(me, lines)
    plane = columns * lines
    depth = HALVES * layers
    spot = column * lines + line
    level = side * layers + layer

    batch, contacts, length = signal_ref.shape
    width = taps_ref.shape[1] - 1
    tokens, patch = tokens_ref.shape
    per_row = length // patch
    total = grads_ref.shape[0]
    half = total // CORES
    piece = half // plane
    has_next = slab < slabs - 1
    has_prior = slab > 0

    def slab_at(column_at, side_at, core_at):
        return (column_at * HALVES + side_at) * CORES + core_at

    core_peer = (slab_at(column, side, 1 - core), me)

    def plane_peer(step):
        at = lax.rem(spot + step, plane)
        return at, (slab_at(at // lines, side, core), layer * lines + lax.rem(at, lines))

    def depth_peer(step):
        at = lax.rem(level + step, depth)
        return slab_at(column, at // layers, core), lax.rem(at, layers) * lines + line

    def contact_peer(step):
        return slab, lax.rem(me + step, members)

    barrier = pltpu.get_barrier_semaphore()

    def greet(device):
        pl.semaphore_signal(barrier, inc=1, device_id=device, device_id_type=MESH)

    def greet_contact(step, carry):
        greet(contact_peer(step))
        return carry

    def greet_plane(step, carry):
        greet(plane_peer(step)[1])
        return carry

    def greet_depth(step, carry):
        greet(depth_peer(step))
        return carry

    lax.fori_loop(1, members, greet_contact, 0)

    @pl.when(has_next)
    def _():
        greet((slab + 1, me))

    @pl.when(has_prior)
    def _():
        greet((slab - 1, me))

    lax.fori_loop(1, plane, greet_plane, 0)
    lax.fori_loop(1, depth, greet_depth, 0)
    greet(core_peer)

    build_tables(taps_ref, table_ref)
    spread_blocks(signal_ref, rows_ref, width)
    run_filter(rows_ref, table_ref, before_ref, own_ref, filtered_ref)

    greetings = members + plane + depth - 2 + has_next.astype(jnp.int32)
    pl.semaphore_wait(barrier, greetings + has_prior.astype(jnp.int32))

    def remote(source, target, which, device):
        return pltpu.make_async_remote_copy(
            src_ref=source,
            dst_ref=target,
            send_sem=send_sem.at[which],
            recv_sem=recv_sem.at[which],
            device_id=device,
            device_id_type=MESH,
        )

    halo = remote(
        signal_ref.at[:, :, pl.ds(length - width, width)],
        halo_ref,
        0,
        (lax.rem(slab + 1, slabs), me),
    )

    @pl.when(has_next)
    def _():
        halo.start()

    def block_of(ref, group):
        return ref.at[
            group // per_row, :, pl.ds(pl.multiple_of(lax.rem(group, per_row) * patch, patch), patch)
        ]

    def rows_of(ref, member):
        return ref.at[pl.ds(pl.multiple_of(member * contacts, contacts), contacts)]

    def send_tokens(peer):
        remote(
            block_of(filtered_ref, peer), rows_of(tokens_ref, me), 2, (slab, peer)
        ).start()

    def send_ready(step, carry):
        peer = lax.rem(me + step, members)

        @pl.when(lax.rem(peer, per_row) != 0)
        def _():
            send_tokens(peer)

        return carry

    def send_upstream(step, carry):
        peer = lax.rem(me + step, members)
        remote(
            block_of(cotangent_ref, peer), rows_of(upstream_ref, me), 1, (slab, peer)
        ).start()
        return carry

    lax.fori_loop(1, members, send_ready, 0)
    lax.fori_loop(1, members, send_upstream, 0)
    own_upstream = pltpu.make_async_copy(
        block_of(cotangent_ref, me), rows_of(upstream_ref, me), local_sem.at[0]
    )
    own_upstream.start()

    @pl.when(has_prior)
    def _():
        halo.wait_recv()

    @pl.when(jnp.logical_not(has_prior))
    def _():
        halo_ref[...] = jnp.zeros_like(halo_ref)

    finish_filter(halo_ref, rows_ref, table_ref, before_ref, own_ref, filtered_ref)

    def send_first(step, carry):
        peer = lax.rem(me // per_row + step, batch) * per_row

        @pl.when(peer != me)
        def _():
            send_tokens(peer)

        return carry

    lax.fori_loop(0, batch, send_first, 0)
    own_tokens = pltpu.make_async_copy(
        block_of(filtered_ref, me), rows_of(tokens_ref, me), local_sem.at[1]
    )
    own_tokens.start()
    count_hits(neighbours_ref, alive_ref, coef_ref, hits_ref, columns_ref)

    def all_but_one(ref, which):
        rest = ref.at[pl.ds(0, (members - 1) * contacts)]
        return remote(rest, rest, which, core_peer)

    tokens_copy = all_but_one(tokens_ref, 2)
    upstream_copy = all_but_one(upstream_ref, 1)
    own_tokens.wait()
    tokens_copy.wait_recv()
    project_tokens(tokens_ref, hits_ref, columns_ref, weights, work)
    own_upstream.wait()
    upstream_copy.wait_recv()
    attend(upstream_ref, columns_ref, weights, work)
    weight_grads(grads_ref, upstream_ref, work, grad_scale)

    other_half = pl.ds(pl.multiple_of((1 - core) * half, half), half)
    my_half = pl.ds(pl.multiple_of(core * half, half), half)
    core_out[...] = grads_ref[other_half, :].astype(BF16)
    core_copy = remote(core_out, core_in, 3, core_peer)
    core_copy.start()

    mixed = work["mixed_t"][...].astype(F32).T.astype(BF16)
    attended_ref[...] = nn(mixed, w_out_ref[...]).astype(BF16)

    core_copy.wait_recv()
    plane_sum[...] = grads_ref[my_half, :] + core_in[...].astype(F32)
    plane_out[...] = plane_sum[...].astype(BF16)

    def piece_of(ref, first, at):
        return ref.at[pl.ds(pl.multiple_of(first + at * piece, piece), piece)]

    def scatter(step, carry):
        at, device = plane_peer(step)
        remote(piece_of(plane_out, 0, at), plane_in.at[step - 1], 4, device).start()
        return carry

    lax.fori_loop(1, plane, scatter, 0)

    def give_back(step, carry):
        peer = lax.rem(me + step, members)
        remote(
            rows_of(attended_ref, peer), block_of(returned_ref, me), 5, (slab, peer)
        ).start()
        return carry

    lax.fori_loop(1, members, give_back, 0)
    own_back = pltpu.make_async_copy(
        rows_of(attended_ref, me), block_of(returned_ref, me), local_sem.at[0]
    )
    own_back.start()

    scatter_copy = remote(plane_in, plane_in, 4, core_peer)
    scatter_copy.wait_recv()
    running = piece_of(plane_sum, 0, spot)[...]
    for step in range(1, plane):
        running = running + plane_in[step - 1].astype(F32)
    depth_in[level] = running.astype(BF16)

    def exchange(step, carry):
        remote(depth_in.at[level], depth_in.at[level], 6, depth_peer(step)).start()
        return carry

    lax.fori_loop(1, depth, exchange, 0)
    rest = depth_in.at[pl.ds(0, depth - 1)]
    depth_copy = remote(rest, rest, 6, core_peer)
    depth_copy.wait_recv()
    running = depth_in[0].astype(F32)
    for at in range(1, depth):
        running = running + depth_in[at].astype(F32)
    own_piece = piece_of(result, core * half, spot)
    own_piece[...] = running.astype(BF16)

    def gather(step, carry):
        remote(own_piece, own_piece, 7, plane_peer(step)[1]).start()
        return carry

    lax.fori_loop(1, plane, gather, 0)
    rest = result.at[pl.ds(0, (plane - 1) * piece)]
    gather_copy = remote(rest, rest, 7, core_peer)
    gather_copy.wait_recv()

    own_half = result.at[my_half]
    last_copy = remote(own_half, own_half, 8, core_peer)
    last_copy.start()
    last_copy.wait_recv()
    summed = pltpu.make_async_copy(result, summed_ref, local_sem.at[1])
    summed.start()

    @pl.when(has_next)
    def _():
        halo.wait_send()

    tokens_copy.wait_send()
    upstream_copy.wait_send()
    core_copy.wait_send()
    scatter_copy.wait_send()
    depth_copy.wait_send()
    gather_copy.wait_send()
    last_copy.wait_send()
    own_back.wait()
    back_copy = all_but_one(attended_ref, 5)
    back_copy.wait_recv()
    back_copy.wait_send()
    summed.wait()


def finish_kernel(returned_ref, summed_ref, out_ref, grads_ref, held, wide_ref, sems):
    parts = held.shape[0]
    rows = held.shape[1]
    back = pltpu.make_async_copy(returned_ref, out_ref, sems.at[0])
    back.start()
    loads = [
        pltpu.make_async_copy(
            summed_ref.at[pl.ds(k * rows, rows)], held.at[k], sems.at[1 + k]
        )
        for k in range(parts)
    ]
    stores = [
        pltpu.make_async_copy(wide_ref.at[k], grads_ref.at[k], sems.at[1 + parts + k])
        for k in range(parts)
    ]
    for load in loads:
        load.start()
    for k in range(parts):
        loads[k].wait()
        wide_ref[k] = held[k].astype(F32)
        stores[k].start()
    for store in stores:
        store.wait()
    back.wait()


VMEM = pl.BlockSpec(memory_space=pltpu.VMEM)
ANY = pl.BlockSpec(memory_space=pl.ANY)


def local(
    signal, fir_taps, neighbours, live_mask, lap_coef, w_query, w_key, w_value, w_out, cotangent
):
    batch, contacts, length = signal.shape
    width = fir_taps.shape[1] - 1
    patch = w_query.shape[0]
    slabs = lax.axis_size("tm")
    members = lax.axis_size("contact")
    tokens = neighbours.shape[0]
    blocks = length // width
    groups = batch * (length // patch) * slabs
    plane = slabs // (CORES * HALVES) * (members // SIDE_LAYERS)
    depth = HALVES * SIDE_LAYERS
    total = 4 * patch
    half = total // CORES
    piece = half // plane
    padded = batch * blocks * contacts
    work = [
        pltpu.VMEM((patch, tokens) if turned else (tokens, patch), dtype)
        for _, turned, dtype in WORK
    ]
    returned, summed = pl.pallas_call(
        functools.partial(step_kernel, slabs, members, (groups * tokens) ** (-0.5)),
        out_shape=(
            jax.ShapeDtypeStruct(signal.shape, BF16),
            jax.ShapeDtypeStruct((total, patch), BF16),
        ),
        in_specs=[VMEM] * 9 + [ANY],
        out_specs=(ANY, ANY),
        scratch_shapes=[
            pltpu.VMEM((batch, contacts, width), BF16),
            pltpu.VMEM((contacts, width, 2 * width), BF16),
            pltpu.VMEM((padded, width), F32),
            pltpu.VMEM((padded, width), F32),
            pltpu.VMEM((padded, width), F32),
            pltpu.VMEM((batch, contacts, length), BF16),
            pltpu.VMEM((tokens, patch), BF16),
            pltpu.VMEM((tokens, patch), BF16),
            pltpu.VMEM((tokens, patch), BF16),
            pltpu.VMEM((tokens, tokens), BF16),
            pltpu.VMEM((4, tokens, 128), F32),
            pltpu.VMEM((total, patch), F32),
            pltpu.VMEM((half, patch), BF16),
            pltpu.VMEM((half, patch), BF16),
            pltpu.VMEM((half, patch), F32),
            pltpu.VMEM((half, patch), BF16),
            pltpu.VMEM((plane - 1, piece, patch), BF16),
            pltpu.VMEM((depth, piece, patch), BF16),
            pltpu.VMEM((total, patch), BF16),
            pltpu.SemaphoreType.DMA((9,)),
            pltpu.SemaphoreType.DMA((9,)),
            pltpu.SemaphoreType.DMA((2,)),
        ]
        + work,
        compiler_params=pltpu.CompilerParams(collective_id=0, has_side_effects=True),
    )(
        signal,
        fir_taps,
        neighbours.T,
        live_mask.reshape(1, tokens),
        lap_coef.reshape(1, tokens),
        w_query,
        w_key,
        w_value,
        w_out,
        cotangent,
    )
    return pl.pallas_call(
        finish_kernel,
        out_shape=(
            jax.ShapeDtypeStruct(signal.shape, BF16),
            jax.ShapeDtypeStruct((4, patch, patch), F32),
        ),
        in_specs=[ANY, ANY],
        out_specs=(ANY, ANY),
        scratch_shapes=[
            pltpu.VMEM((4, patch, patch), BF16),
            pltpu.VMEM((4, patch, patch), F32),
            pltpu.SemaphoreType.DMA((9,)),
        ],
    )(returned, summed)


def solution(mesh):
    in_specs = (
        P(None, "contact", "tm"),
        P("contact", None),
        P(),
        P(),
        P(),
        P(),
        P(),
        P(),
        P(),
        P(None, "contact", "tm"),
    )
    out_specs = (P(None, "contact", "tm"), P())
    return jax.shard_map(local, mesh=mesh, in_specs=in_specs, out_specs=out_specs, check_vma=False)
```

time: 491 us -> 77.5 us (0.16)
  waiting for transfers between devices: 262 us -> 0 us
  local copies, waits for them, and re-layouts: 141 us -> 0 us
  Pallas kernels: 0 us -> 76.7 us
  starting transfers between devices: 39 us -> 0 us
  blocking collectives: 14.6 us -> 0 us
  between operations: 14.6 us -> 0.64 us
  matrix products: 10.1 us -> 0 us
  other arithmetic: 9.12 us -> 0 us
    psum x1 -> x0, waiting for transfers between devices: 250 us -> none  [local(): summed = lax.psum(running, ('tm', 'contact'))]
    gather x4 -> x0, local copies, waits for them, and re-layouts: 134 us -> none  [the longest x2 121 us: toeplitz(): picked = jnp.take(fir_taps, jnp.clip(lag_table, 0, rim_width), axis=1)]
    pallas_call x0 -> x2, Pallas kernels: none -> 76.7 us  [the longest x1 67.6 us: local(): pl.pallas_call(functools.partial(step_kernel, slabs, members, (groups * t...]
    all_to_all x2 -> x0, starting transfers between devices: 21.4 us -> none  [the longest x1 11.5 us: local(): lax.all_to_all(grouped, 'contact', split_axis=0, concat_axis=1, tiled=True)]
    ppermute x3 -> x0, starting transfers between devices: 17.3 us -> none  [the longest x1 12 us: from_behind(): return lax.ppermute(value, axis, pairs)]
    all_to_all x1 -> x0, blocking collectives: 14.6 us -> none  [local(): lax.all_to_all(attended_groups, 'contact', split_axis=1, concat_axis=0, t...]
    dot_general x35 -> x0, matrix products: 10.1 us -> none  [the longest x21 6.61 us: contract(): lax.dot_general(left, right, (((left_dim,), (right_dim,)), ((), ())), pre...]
    all_to_all x2 -> x0, waiting for transfers between devices: 9.54 us -> none  [the longest x1 9.54 us: local(): lax.all_to_all(grouped, 'contact', split_axis=0, concat_axis=1, tiled=True)]
  transfers between devices with their start and end apart: 6 -> 0, of which waited for: 4 -> 0; matrix products, arithmetic and copies ran while one was open for 30% -> 0% of each run, Pallas kernels for 0% -> 0%
where the time goes in v1:
time: 77.5 us; the launch traced here: 77.4 us
  Pallas kernels  76.7 us (99%)
    pallas_call x1, Pallas kernels, local(): pl.pallas_call(functools.partial(step_kernel, slabs, members, (groups * t...  67.6 us
    pallas_call x1, Pallas kernels, local(): pl.pallas_call(finish_kernel, out_shape=(jax.ShapeDtypeStruct(signal.shap...  9.12 us

profile of v1, /device:TPU:1, one launch (start us, length us, event | category | flops | bytes accessed | tf_op | source)
XLA Modules:
  0.0 77.4 jit_solution(734755235424113628)
XLA Ops:
  0.6 67.6 %shard_map.113 = (bf16[8,16,1024]{2,1,0:T(8,128)(2,1)}, bf16[1024,256]{1,0:T(8,128)(2,1)}) custom-call(bf16[8,16,1024]{2,1,0:T(8,128)(2,1)} %signal_ref.1, bf16[16,129]{1,0:T(8,128)(2,1)} %taps_ref.1, s32[4,512]{1,0:T(4,128)} %bitcast.3, s32[1,512]{1,0:T(1,128)} %bitcast.4, f32[1,512]{1,0:T(1,128)} %bitcast.5, bf16[256,256]{1,0:T(8,128)(2,1)} %w_query_ref.1, ...), custom_call_target="tpu_custom_call" | custom-call | tf_op jit(solution)/shard_map/pallas_call | solution.py:571
  68.3 9.1 %shard_map.114 = (bf16[8,16,1024]{2,1,0:T(8,128)(2,1)}, f32[4,256,256]{2,1,0:T(8,128)}) custom-call(bf16[8,16,1024]{2,1,0:T(8,128)(2,1)} %get-tuple-element.4.returned_ref, bf16[1024,256]{1,0:T(8,128)(2,1)} %get-tuple-element.5.summed_ref), custom_call_target="tpu_custom_call" | custom-call | tf_op jit(solution)/shard_map/pallas_call | solution.py:617

commit v2 on v1

--- a/solution.py
+++ b/solution.py
@@ -11,6 +11,7 @@
 CORES = 2
 HALVES = 2
 SIDE_LAYERS = 4
+VMEM_BYTES = 32 * 2**20
 MESH = pl.DeviceIdType.MESH
 F32 = jnp.float32
 BF16 = jnp.bfloat16
@@ -212,6 +213,18 @@
     slabs,
     members,
     grad_scale,
+    signal_hbm,
+    taps_hbm,
+    neighbours_hbm,
+    alive_hbm,
+    coef_hbm,
+    w_query_hbm,
+    w_key_hbm,
+    w_value_hbm,
+    w_out_hbm,
+    cotangent_ref,
+    returned_ref,
+    summed_ref,
     signal_ref,
     taps_ref,
     neighbours_ref,
@@ -221,9 +234,6 @@
     w_key_ref,
     w_value_ref,
     w_out_ref,
-    cotangent_ref,
-    returned_ref,
-    summed_ref,
     halo_ref,
     table_ref,
     rows_ref,
@@ -246,8 +256,27 @@
     send_sem,
     recv_sem,
     local_sem,
+    load_sem,
     *work_refs,
 ):
+    loads = [
+        pltpu.make_async_copy(source, target, load_sem.at[k])
+        for k, (source, target) in enumerate(
+            (
+                (signal_hbm, signal_ref),
+                (taps_hbm, taps_ref),
+                (neighbours_hbm, neighbours_ref),
+                (alive_hbm, alive_ref),
+                (coef_hbm, coef_ref),
+                (w_query_hbm, w_query_ref),
+                (w_key_hbm, w_key_ref),
+                (w_value_hbm, w_value_ref),
+                (w_out_hbm, w_out_ref),
+            )
+        )
+    ]
+    for load in loads:
+        load.start()
     work = {entry[0]: ref for entry, ref in zip(WORK, work_refs)}
     weights = (w_query_ref, w_key_ref, w_value_ref, w_out_ref)
     slab = lax.axis_index("tm")
@@ -308,8 +337,6 @@
         greet(depth_peer(step))
         return carry
 
-    lax.fori_loop(1, members, greet_contact, 0)
-
     @pl.when(has_next)
     def _():
         greet((slab + 1, me))
@@ -318,10 +345,13 @@
     def _():
         greet((slab - 1, me))
 
+    lax.fori_loop(1, members, greet_contact, 0)
     lax.fori_loop(1, plane, greet_plane, 0)
     lax.fori_loop(1, depth, greet_depth, 0)
     greet(core_peer)
 
+    for load in loads:
+        load.wait()
     build_tables(taps_ref, table_ref)
     spread_blocks(signal_ref, rows_ref, width)
     run_filter(rows_ref, table_ref, before_ref, own_ref, filtered_ref)
@@ -439,16 +469,28 @@
     plane_sum[...] = grads_ref[my_half, :] + core_in[...].astype(F32)
     plane_out[...] = plane_sum[...].astype(BF16)
 
-    def piece_of(ref, first, at):
-        return ref.at[pl.ds(pl.multiple_of(first + at * piece, piece), piece)]
+    def piece_of(ref, at):
+        return ref.at[pl.ds(pl.multiple_of(at * piece, piece), piece)]
 
     def scatter(step, carry):
         at, device = plane_peer(step)
-        remote(piece_of(plane_out, 0, at), plane_in.at[step - 1], 4, device).start()
+        remote(piece_of(plane_out, at), plane_in.at[step - 1], 4, device).start()
         return carry
 
     lax.fori_loop(1, plane, scatter, 0)
 
+    scatter_copy = remote(plane_in, plane_in, 4, core_peer)
+    scatter_copy.wait_recv()
+    running = piece_of(plane_sum, spot)[...]
+    for step in range(1, plane):
+        running = running + plane_in[step - 1].astype(F32)
+    depth_in[level] = running.astype(BF16)
+
+    def exchange(step, carry):
+        remote(depth_in.at[level], depth_in.at[level], 6, depth_peer(step)).start()
+        return carry
+
+    lax.fori_loop(1, depth, exchange, 0)
     def give_back(step, carry):
         peer = lax.rem(me + step, members)
         remote(
@@ -462,25 +504,13 @@
     )
     own_back.start()
 
-    scatter_copy = remote(plane_in, plane_in, 4, core_peer)
-    scatter_copy.wait_recv()
-    running = piece_of(plane_sum, 0, spot)[...]
-    for step in range(1, plane):
-        running = running + plane_in[step - 1].astype(F32)
-    depth_in[level] = running.astype(BF16)
-
-    def exchange(step, carry):
-        remote(depth_in.at[level], depth_in.at[level], 6, depth_peer(step)).start()
-        return carry
-
-    lax.fori_loop(1, depth, exchange, 0)
     rest = depth_in.at[pl.ds(0, depth - 1)]
     depth_copy = remote(rest, rest, 6, core_peer)
     depth_copy.wait_recv()
     running = depth_in[0].astype(F32)
     for at in range(1, depth):
         running = running + depth_in[at].astype(F32)
-    own_piece = piece_of(result, core * half, spot)
+    own_piece = piece_of(result, spot)
     own_piece[...] = running.astype(BF16)
 
     def gather(step, carry):
@@ -492,12 +522,11 @@
     gather_copy = remote(rest, rest, 7, core_peer)
     gather_copy.wait_recv()
 
-    own_half = result.at[my_half]
-    last_copy = remote(own_half, own_half, 8, core_peer)
+    last_copy = remote(result, summed_ref.at[my_half], 8, core_peer)
     last_copy.start()
+    summed = pltpu.make_async_copy(result, summed_ref.at[my_half], local_sem.at[1])
+    summed.start()
     last_copy.wait_recv()
-    summed = pltpu.make_async_copy(result, summed_ref, local_sem.at[1])
-    summed.start()
 
     @pl.when(has_next)
     def _():
@@ -517,34 +546,9 @@
     summed.wait()
 
 
-def finish_kernel(returned_ref, summed_ref, out_ref, grads_ref, held, wide_ref, sems):
-    parts = held.shape[0]
-    rows = held.shape[1]
-    back = pltpu.make_async_copy(returned_ref, out_ref, sems.at[0])
-    back.start()
-    loads = [
-        pltpu.make_async_copy(
-            summed_ref.at[pl.ds(k * rows, rows)], held.at[k], sems.at[1 + k]
-        )
-        for k in range(parts)
-    ]
-    stores = [
-        pltpu.make_async_copy(wide_ref.at[k], grads_ref.at[k], sems.at[1 + parts + k])
-        for k in range(parts)
-    ]
-    for load in loads:
-        load.start()
-    for k in range(parts):
-        loads[k].wait()
-        wide_ref[k] = held[k].astype(F32)
-        stores[k].start()
-    for store in stores:
-        store.wait()
-    back.wait()
-
-
 VMEM = pl.BlockSpec(memory_space=pltpu.VMEM)
 ANY = pl.BlockSpec(memory_space=pl.ANY)
+HBM = pl.BlockSpec(memory_space=pltpu.HBM)
 
 
 def local(
@@ -574,9 +578,18 @@
             jax.ShapeDtypeStruct(signal.shape, BF16),
             jax.ShapeDtypeStruct((total, patch), BF16),
         ),
-        in_specs=[VMEM] * 9 + [ANY],
+        in_specs=[HBM] * 10,
         out_specs=(ANY, ANY),
         scratch_shapes=[
+            pltpu.VMEM(signal.shape, BF16),
+            pltpu.VMEM(fir_taps.shape, BF16),
+            pltpu.VMEM((neighbours.shape[1], tokens), jnp.int32),
+            pltpu.VMEM((1, tokens), jnp.int32),
+            pltpu.VMEM((1, tokens), F32),
+            pltpu.VMEM((patch, patch), BF16),
+            pltpu.VMEM((patch, patch), BF16),
+            pltpu.VMEM((patch, patch), BF16),
+            pltpu.VMEM((patch, patch), BF16),
             pltpu.VMEM((batch, contacts, width), BF16),
             pltpu.VMEM((contacts, width, 2 * width), BF16),
             pltpu.VMEM((padded, width), F32),
@@ -595,39 +608,34 @@
             pltpu.VMEM((half, patch), BF16),
             pltpu.VMEM((plane - 1, piece, patch), BF16),
             pltpu.VMEM((depth, piece, patch), BF16),
-            pltpu.VMEM((total, patch), BF16),
+            pltpu.VMEM((half, patch), BF16),
             pltpu.SemaphoreType.DMA((9,)),
             pltpu.SemaphoreType.DMA((9,)),
             pltpu.SemaphoreType.DMA((2,)),
+            pltpu.SemaphoreType.DMA((9,)),
         ]
         + work,
-        compiler_params=pltpu.CompilerParams(collective_id=0, has_side_effects=True),
+        compiler_params=pltpu.CompilerParams(
+            collective_id=0, has_side_effects=True, vmem_limit_bytes=VMEM_BYTES
+        ),
     )(
-        signal,
-        fir_taps,
-        neighbours.T,
-        live_mask.reshape(1, tokens),
-        lap_coef.reshape(1, tokens),
-        w_query,
-        w_key,
-        w_value,
-        w_out,
-        cotangent,
-    )
-    return pl.pallas_call(
-        finish_kernel,
-        out_shape=(
-            jax.ShapeDtypeStruct(signal.shape, BF16),
-            jax.ShapeDtypeStruct((4, patch, patch), F32),
-        ),
-        in_specs=[ANY, ANY],
-        out_specs=(ANY, ANY),
-        scratch_shapes=[
-            pltpu.VMEM((4, patch, patch), BF16),
-            pltpu.VMEM((4, patch, patch), F32),
-            pltpu.SemaphoreType.DMA((9,)),
-        ],
-    )(returned, summed)
+        *(
+            pltpu.with_memory_space_constraint(array, pltpu.HBM)
+            for array in (
+                signal,
+                fir_taps,
+                neighbours.T,
+                live_mask.reshape(1, tokens),
+                lap_coef.reshape(1, tokens),
+                w_query,
+                w_key,
+                w_value,
+                w_out,
+                cotangent,
+            )
+        )
+    )
+    return (returned, summed.astype(F32).reshape(4, patch, patch))
 
 
 def solution(mesh):

time: 77.5 us -> 70.3 us (0.907)
  Pallas kernels: 76.7 us -> 67.8 us
  other arithmetic: 0 us -> 1.06 us
    pallas_call x1 -> x0, Pallas kernels: 9.12 us -> none  [local(): pl.pallas_call(finish_kernel, out_shape=(jax.ShapeDtypeStruct(signal.shap...]
    reshape x0 -> x1, other arithmetic: none -> 1.06 us  [local(): return (returned, summed.astype(F32).reshape(4, patch, patch))]
where the time goes in v2:
time: 70.3 us; the launch traced here: 70.2 us
  Pallas kernels  67.8 us (96%)
  other arithmetic  1.06 us (2%)
    pallas_call x1, Pallas kernels, local(): pl.pallas_call(functools.partial(step_kernel, slabs, members, (groups * t...  67.8 us

profile of v2, /device:TPU:1, one launch (start us, length us, event | category | flops | bytes accessed | tf_op | source)
XLA Modules:
  0.0 70.2 jit_solution(10816513942113267556)
XLA Ops:
  0.6 67.8 %shard_map.113 = (bf16[8,16,1024]{2,1,0:T(8,128)(2,1)S(1)}, bf16[1024,256]{1,0:T(8,128)(2,1)S(1)}) custom-call(bf16[8,16,1024]{2,1,0:T(8,128)(2,1)} %signal_hbm.1, bf16[16,129]{1,0:T(8,128)(2,1)} %taps_hbm.1, s32[4,512]{1,0:T(4,128)} %bitcast.6, s32[1,512]{1,0:T(1,128)} %bitcast.7, f32[1,512]{1,0:T(1,128)} %bitcast.8, bf16[256,256]{1,0:T(8,128)(2,1)} %w_query_hbm.1, ...), custom_call_target="tpu_custom_call" | custom-call | tf_op jit(solution)/shard_map/pallas_call | solution.py:575
  68.4 1.1 %convert.1 = f32[4,256,256]{2,1,0:T(8,128)} convert(bf16[4,256,256]{2,1,0:T(8,128)(2,1)S(1)} %bitcast.5) | non-fusion elementwise | flops 262144 | bytes 1572864 | tf_op jit(solution)/shard_map/reshape | solution.py:638
  69.5 0.7 %copy.13 = bf16[8,16,1024]{2,1,0:T(8,128)(2,1)} copy(bf16[8,16,1024]{2,1,0:T(8,128)(2,1)S(1)} %get-tuple-element.8) | data formatting | bytes 524288

commit v3 on v2

--- a/solution.py
+++ b/solution.py
@@ -137,60 +137,79 @@
     work["value_t"][...] = values.astype(F32).T.astype(BF16)
 
 
-def attend(upstream_ref, columns_ref, weights, work):
-    w_out_ref = weights[3]
-    tokens, patch = upstream_ref.shape
+def head_slices(patch, h):
     head = patch // HEADS
-    score_scale = head ** (-0.5)
+    pair = 2 * head
+    return slice(h // 2 * pair, h // 2 * pair + pair), slice(h * head, (h + 1) * head)
+
+
+def one_of_pair(ref, h):
+    tokens, patch = ref.shape
+    head = patch // HEADS
+    at, _ = head_slices(patch, h)
+    lane = lax.broadcasted_iota(jnp.int32, (tokens, 2 * head), 1)
+    inside = lane < head if h % 2 == 0 else lane >= head
+    return jnp.where(inside, ref[:, at].astype(F32), 0.0).astype(BF16)
+
+
+def attend(columns_ref, work):
+    tokens, patch = work["key"].shape
+    bias = wide(columns_ref[3], tokens)
+    for h in range(HEADS):
+        at, rows = head_slices(patch, h)
+        scores = nt(work["key"][:, at], one_of_pair(work["query"], h)) + bias
+        raised = jnp.exp(scores - jnp.max(scores, axis=0, keepdims=True))
+        prob = raised * (1.0 / jnp.sum(raised, axis=0, keepdims=True))
+        prob_low = prob.astype(BF16)
+        work["prob"][h] = prob
+        work["prob_low"][h] = prob_low
+        work["mixed_t"][rows, :] = nn(work["value_t"][rows, :], prob_low).astype(BF16)
+
+
+def emit_attended(attended_ref, w_out_ref, work):
+    mixed = work["mixed_t"][...].astype(F32).T.astype(BF16)
+    attended_ref[...] = nn(mixed, w_out_ref[...]).astype(BF16)
+
+
+def value_grads(upstream_ref, w_out_ref, work):
+    patch = upstream_ref.shape[1]
     back = nt(upstream_ref[...], w_out_ref[...]).astype(BF16)
     work["back"][...] = back
-    work["back_t"][...] = back.astype(F32).T
-    pair = 2 * head
-    lane = lax.broadcasted_iota(jnp.int32, (tokens, pair), 1)
-    bias = wide(columns_ref[3], tokens)
-    for p in range(HEADS // 2):
-        at = slice(p * pair, (p + 1) * pair)
-        grad_key = None
-        grad_value = None
-        for s in range(2):
-            h = 2 * p + s
-            rows = slice(h * head, (h + 1) * head)
-            inside = (lane >= s * head) & (lane < (s + 1) * head)
-            query = jnp.where(inside, work["query"][:, at].astype(F32), 0.0).astype(BF16)
-            backward = jnp.where(inside, work["back"][:, at].astype(F32), 0.0).astype(BF16)
-            scores = nt(work["key"][:, at], query) + bias
-            raised = jnp.exp(scores - jnp.max(scores, axis=0, keepdims=True))
-            prob = raised * (1.0 / jnp.sum(raised, axis=0, keepdims=True))
-            prob_low = prob.astype(BF16)
-            mixed_t = nn(work["value_t"][rows, :], prob_low).astype(BF16)
-            work["mixed_t"][rows, :] = mixed_t
-            inner = jnp.sum(
-                work["back_t"][rows, :] * mixed_t.astype(F32), axis=0, keepdims=True
+    back_t = back.astype(F32).T
+    for h in range(0, HEADS, 2):
+        at, _ = head_slices(patch, h)
+        total = None
+        for one in (h, h + 1):
+            _, rows = head_slices(patch, one)
+            work["inner"][one] = jnp.sum(
+                back_t[rows] * work["mixed_t"][rows, :].astype(F32), axis=0, keepdims=True
             )
-            grad_prob = nt(work["value"][:, at], backward)
-            grad_score = (prob * (grad_prob - inner)).astype(BF16)
-            part_value = nn(prob_low, backward)
-            part_key = nn(grad_score, query)
-            grad_value = part_value if s == 0 else grad_value + part_value
-            grad_key = part_key if s == 0 else grad_key + part_key
-            work["grad_query_t"][rows, :] = (
-                nn(work["key_t"][rows, :], grad_score) * score_scale
-            ).astype(BF16)
-        work["grad_key"][:, at] = grad_key.astype(BF16)
-        work["grad_value"][:, at] = grad_value.astype(BF16)
-
-
-def weight_grads(grads_ref, upstream_ref, work, grad_scale):
-    patch = upstream_ref.shape[1]
-    normed_t = work["normed_t"][...]
-    products = (
-        nt(normed_t, work["grad_query_t"][...]),
-        nn(normed_t, work["grad_key"][...]),
-        nn(normed_t, work["grad_value"][...]),
-        nn(work["mixed_t"][...], upstream_ref[...]),
-    )
+            part = nn(work["prob_low"][one], one_of_pair(work["back"], one))
+            total = part if total is None else total + part
+        work["grad_value"][:, at] = total.astype(BF16)
+
+
+def score_grads(pair, work):
+    tokens, patch = work["key"].shape
+    score_scale = (patch // HEADS) ** (-0.5)
+    total = None
+    for h in (2 * pair, 2 * pair + 1):
+        at, rows = head_slices(patch, h)
+        grad_prob = nt(work["value"][:, at], one_of_pair(work["back"], h))
+        grad_score = (work["prob"][h] * (grad_prob - work["inner"][h])).astype(BF16)
+        part = nn(grad_score, one_of_pair(work["query"], h))
+        total = part if total is None else total + part
+        work["grad_query_t"][rows, :] = (
+            nn(work["key_t"][rows, :], grad_score) * score_scale
+        ).astype(BF16)
+    work["grad_key"][:, at] = total.astype(BF16)
+
+
+def store_grads(grads_ref, products, grad_scale):
+    rows = products[0].shape[0]
+    pieces, piece = grads_ref.shape[1:3]
     for k, product in enumerate(products):
-        grads_ref[k * patch : (k + 1) * patch, :] = product * grad_scale
+        grads_ref[k] = (product * grad_scale).reshape(pieces, piece, product.shape[1])
 
 
 WORK = (
@@ -202,7 +221,6 @@
     ("grad_value", 0, BF16),
     ("key_t", 1, BF16),
     ("value_t", 1, BF16),
-    ("back_t", 1, F32),
     ("normed_t", 1, BF16),
     ("mixed_t", 1, BF16),
     ("grad_query_t", 1, BF16),
@@ -253,6 +271,9 @@
     plane_in,
     depth_in,
     result,
+    prob_ref,
+    prob_low_ref,
+    inner_ref,
     send_sem,
     recv_sem,
     local_sem,
@@ -278,6 +299,9 @@
     for load in loads:
         load.start()
     work = {entry[0]: ref for entry, ref in zip(WORK, work_refs)}
+    work["prob"] = prob_ref
+    work["prob_low"] = prob_low_ref
+    work["inner"] = inner_ref
     weights = (w_query_ref, w_key_ref, w_value_ref, w_out_ref)
     slab = lax.axis_index("tm")
     me = lax.axis_index("contact")
@@ -298,9 +322,6 @@
     width = taps_ref.shape[1] - 1
     tokens, patch = tokens_ref.shape
     per_row = length // patch
-    total = grads_ref.shape[0]
-    half = total // CORES
-    piece = half // plane
     has_next = slab < slabs - 1
     has_prior = slab > 0
 
@@ -409,8 +430,9 @@
         ).start()
         return carry
 
+    early = members // 2
     lax.fori_loop(1, members, send_ready, 0)
-    lax.fori_loop(1, members, send_upstream, 0)
+    lax.fori_loop(1, early, send_upstream, 0)
     own_upstream = pltpu.make_async_copy(
         block_of(cotangent_ref, me), rows_of(upstream_ref, me), local_sem.at[0]
     )
@@ -436,6 +458,7 @@
         return carry
 
     lax.fori_loop(0, batch, send_first, 0)
+    lax.fori_loop(early, members, send_upstream, 0)
     own_tokens = pltpu.make_async_copy(
         block_of(filtered_ref, me), rows_of(tokens_ref, me), local_sem.at[1]
     )
@@ -451,82 +474,120 @@
     own_tokens.wait()
     tokens_copy.wait_recv()
     project_tokens(tokens_ref, hits_ref, columns_ref, weights, work)
-    own_upstream.wait()
-    upstream_copy.wait_recv()
-    attend(upstream_ref, columns_ref, weights, work)
-    weight_grads(grads_ref, upstream_ref, work, grad_scale)
-
-    other_half = pl.ds(pl.multiple_of((1 - core) * half, half), half)
-    my_half = pl.ds(pl.multiple_of(core * half, half), half)
-    core_out[...] = grads_ref[other_half, :].astype(BF16)
-    core_copy = remote(core_out, core_in, 3, core_peer)
-    core_copy.start()
-
-    mixed = work["mixed_t"][...].astype(F32).T.astype(BF16)
-    attended_ref[...] = nn(mixed, w_out_ref[...]).astype(BF16)
-
-    core_copy.wait_recv()
-    plane_sum[...] = grads_ref[my_half, :] + core_in[...].astype(F32)
-    plane_out[...] = plane_sum[...].astype(BF16)
-
-    def piece_of(ref, at):
-        return ref.at[pl.ds(pl.multiple_of(at * piece, piece), piece)]
-
-    def scatter(step, carry):
-        at, device = plane_peer(step)
-        remote(piece_of(plane_out, at), plane_in.at[step - 1], 4, device).start()
-        return carry
-
-    lax.fori_loop(1, plane, scatter, 0)
-
-    scatter_copy = remote(plane_in, plane_in, 4, core_peer)
-    scatter_copy.wait_recv()
-    running = piece_of(plane_sum, spot)[...]
-    for step in range(1, plane):
-        running = running + plane_in[step - 1].astype(F32)
-    depth_in[level] = running.astype(BF16)
-
-    def exchange(step, carry):
-        remote(depth_in.at[level], depth_in.at[level], 6, depth_peer(step)).start()
-        return carry
-
-    lax.fori_loop(1, depth, exchange, 0)
+    attend(columns_ref, work)
+    emit_attended(attended_ref, w_out_ref, work)
+
     def give_back(step, carry):
         peer = lax.rem(me + step, members)
         remote(
-            rows_of(attended_ref, peer), block_of(returned_ref, me), 5, (slab, peer)
+            rows_of(attended_ref, peer), block_of(returned_ref, me), 3, (slab, peer)
         ).start()
         return carry
 
     lax.fori_loop(1, members, give_back, 0)
     own_back = pltpu.make_async_copy(
-        rows_of(attended_ref, me), block_of(returned_ref, me), local_sem.at[0]
+        rows_of(attended_ref, me), block_of(returned_ref, me), local_sem.at[2]
     )
     own_back.start()
 
-    rest = depth_in.at[pl.ds(0, depth - 1)]
-    depth_copy = remote(rest, rest, 6, core_peer)
-    depth_copy.wait_recv()
-    running = depth_in[0].astype(F32)
-    for at in range(1, depth):
-        running = running + depth_in[at].astype(F32)
-    own_piece = piece_of(result, spot)
-    own_piece[...] = running.astype(BF16)
-
-    def gather(step, carry):
-        remote(own_piece, own_piece, 7, plane_peer(step)[1]).start()
-        return carry
-
-    lax.fori_loop(1, plane, gather, 0)
-    rest = result.at[pl.ds(0, (plane - 1) * piece)]
-    gather_copy = remote(rest, rest, 7, core_peer)
-    gather_copy.wait_recv()
-
-    last_copy = remote(result, summed_ref.at[my_half], 8, core_peer)
-    last_copy.start()
-    summed = pltpu.make_async_copy(result, summed_ref.at[my_half], local_sem.at[1])
-    summed.start()
-    last_copy.wait_recv()
+    def core_copy(part):
+        return remote(core_out.at[part], core_in.at[part], 4 + 5 * part, core_peer)
+
+    def scatter_copy(part):
+        ref = plane_in.at[part]
+        return remote(ref, ref, 5 + 5 * part, core_peer)
+
+    def depth_copy(part):
+        rest = depth_in.at[part, pl.ds(0, depth - 1)]
+        return remote(rest, rest, 6 + 5 * part, core_peer)
+
+    def gather_copy(part):
+        rest = result.at[part, pl.ds(0, plane - 1)]
+        return remote(rest, rest, 7 + 5 * part, core_peer)
+
+    def last_copy(part):
+        return remote(
+            result.at[part], summed_ref.at[part, core], 8 + 5 * part, core_peer
+        )
+
+    def own_summed(part):
+        return pltpu.make_async_copy(
+            result.at[part], summed_ref.at[part, core], local_sem.at[part]
+        )
+
+    def start_core(part, products):
+        store_grads(grads_ref.at[part], products, grad_scale)
+        core_out[part] = grads_ref[part, 1 - core].astype(BF16)
+        core_copy(part).start()
+
+    def start_scatter(part):
+        core_copy(part).wait_recv()
+        both = grads_ref[part, core] + core_in[part].astype(F32)
+        plane_sum[part] = both
+        plane_out[part] = both.astype(BF16)
+
+        def scatter(step, carry):
+            at, device = plane_peer(step)
+            remote(
+                plane_out.at[part, at], plane_in.at[part, step - 1], 5 + 5 * part, device
+            ).start()
+            return carry
+
+        lax.fori_loop(1, plane, scatter, 0)
+
+    def start_exchange(part):
+        scatter_copy(part).wait_recv()
+        running = plane_sum[part, spot]
+        for step in range(1, plane):
+            running = running + plane_in[part, step - 1].astype(F32)
+        depth_in[part, level] = running.astype(BF16)
+        own = depth_in.at[part, level]
+
+        def exchange(step, carry):
+            remote(own, own, 6 + 5 * part, depth_peer(step)).start()
+            return carry
+
+        lax.fori_loop(1, depth, exchange, 0)
+
+    def start_gather(part):
+        depth_copy(part).wait_recv()
+        running = depth_in[part, 0].astype(F32)
+        for at in range(1, depth):
+            running = running + depth_in[part, at].astype(F32)
+        result[part, spot] = running.astype(BF16)
+        own = result.at[part, spot]
+
+        def gather(step, carry):
+            remote(own, own, 7 + 5 * part, plane_peer(step)[1]).start()
+            return carry
+
+        lax.fori_loop(1, plane, gather, 0)
+
+    def start_last(part):
+        gather_copy(part).wait_recv()
+        last_copy(part).start()
+        own_summed(part).start()
+
+    own_upstream.wait()
+    upstream_copy.wait_recv()
+    value_grads(upstream_ref, w_out_ref, work)
+    normed_t = work["normed_t"][...]
+    start_core(
+        1, (nn(normed_t, work["grad_value"][...]), nn(work["mixed_t"][...], upstream_ref[...]))
+    )
+    score_grads(0, work)
+    start_scatter(1)
+    score_grads(1, work)
+    start_core(
+        0, (nt(normed_t, work["grad_query_t"][...]), nn(normed_t, work["grad_key"][...]))
+    )
+    start_scatter(0)
+    start_exchange(1)
+    start_exchange(0)
+    start_gather(1)
+    start_gather(0)
+    start_last(1)
+    start_last(0)
 
     @pl.when(has_next)
     def _():
@@ -534,16 +595,19 @@
 
     tokens_copy.wait_send()
     upstream_copy.wait_send()
-    core_copy.wait_send()
-    scatter_copy.wait_send()
-    depth_copy.wait_send()
-    gather_copy.wait_send()
-    last_copy.wait_send()
+    for part in range(2):
+        core_copy(part).wait_send()
+        scatter_copy(part).wait_send()
+        depth_copy(part).wait_send()
+        gather_copy(part).wait_send()
+        last_copy(part).wait_send()
     own_back.wait()
-    back_copy = all_but_one(attended_ref, 5)
+    back_copy = all_but_one(attended_ref, 3)
     back_copy.wait_recv()
     back_copy.wait_send()
-    summed.wait()
+    for part in range(2):
+        last_copy(part).wait_recv()
+        own_summed(part).wait()
 
 
 VMEM = pl.BlockSpec(memory_space=pltpu.VMEM)
@@ -564,9 +628,8 @@
     groups = batch * (length // patch) * slabs
     plane = slabs // (CORES * HALVES) * (members // SIDE_LAYERS)
     depth = HALVES * SIDE_LAYERS
-    total = 4 * patch
-    half = total // CORES
-    piece = half // plane
+    piece = 2 * patch // CORES // plane
+    pieces = (2, plane, piece, patch)
     padded = batch * blocks * contacts
     work = [
         pltpu.VMEM((patch, tokens) if turned else (tokens, patch), dtype)
@@ -576,7 +639,7 @@
         functools.partial(step_kernel, slabs, members, (groups * tokens) ** (-0.5)),
         out_shape=(
             jax.ShapeDtypeStruct(signal.shape, BF16),
-            jax.ShapeDtypeStruct((total, patch), BF16),
+            jax.ShapeDtypeStruct((2, CORES, plane, piece, patch), BF16),
         ),
         in_specs=[HBM] * 10,
         out_specs=(ANY, ANY),
@@ -601,17 +664,20 @@
             pltpu.VMEM((tokens, patch), BF16),
             pltpu.VMEM((tokens, tokens), BF16),
             pltpu.VMEM((4, tokens, 128), F32),
-            pltpu.VMEM((total, patch), F32),
-            pltpu.VMEM((half, patch), BF16),
-            pltpu.VMEM((half, patch), BF16),
-            pltpu.VMEM((half, patch), F32),
-            pltpu.VMEM((half, patch), BF16),
-            pltpu.VMEM((plane - 1, piece, patch), BF16),
-            pltpu.VMEM((depth, piece, patch), BF16),
-            pltpu.VMEM((half, patch), BF16),
-            pltpu.SemaphoreType.DMA((9,)),
-            pltpu.SemaphoreType.DMA((9,)),
-            pltpu.SemaphoreType.DMA((2,)),
+            pltpu.VMEM((2, CORES, plane, piece, patch), F32),
+            pltpu.VMEM(pieces, BF16),
+            pltpu.VMEM(pieces, BF16),
+            pltpu.VMEM(pieces, F32),
+            pltpu.VMEM(pieces, BF16),
+            pltpu.VMEM((2, plane - 1, piece, patch), BF16),
+            pltpu.VMEM((2, depth, piece, patch), BF16),
+            pltpu.VMEM(pieces, BF16),
+            pltpu.VMEM((HEADS, tokens, tokens), F32),
+            pltpu.VMEM((HEADS, tokens, tokens), BF16),
+            pltpu.VMEM((HEADS, 1, tokens), F32),
+            pltpu.SemaphoreType.DMA((14,)),
+            pltpu.SemaphoreType.DMA((14,)),
+            pltpu.SemaphoreType.DMA((3,)),
             pltpu.SemaphoreType.DMA((9,)),
         ]
         + work,

time: 70.3 us -> 65.3 us (0.929)
  Pallas kernels: 67.8 us -> 62.8 us
    pallas_call x1, Pallas kernels: 67.8 us -> 62.8 us  [local(): pl.pallas_call(functools.partial(step_kernel, slabs, members, (groups * t...]
where the time goes in v3:
time: 65.3 us; the launch traced here: 65.2 us
  Pallas kernels  62.8 us (96%)
  other arithmetic  1.06 us (2%)
  local copies, waits for them, and re-layouts  0.7 us (1%)
    pallas_call x1, Pallas kernels, local(): pl.pallas_call(functools.partial(step_kernel, slabs, members, (groups * t...  62.8 us

profile of v3, /device:TPU:1, one launch (start us, length us, event | category | flops | bytes accessed | tf_op | source)
XLA Modules:
  0.0 65.2 jit_solution(17671129474393727917)
XLA Ops:
  0.6 62.8 %shard_map.113 = (bf16[8,16,1024]{2,1,0:T(8,128)(2,1)S(1)}, bf16[2,2,32,8,256]{4,3,2,1,0:T(8,128)(2,1)S(1)}) custom-call(bf16[8,16,1024]{2,1,0:T(8,128)(2,1)} %signal_hbm.1, bf16[16,129]{1,0:T(8,128)(2,1)} %taps_hbm.1, s32[4,512]{1,0:T(4,128)} %bitcast.6, s32[1,512]{1,0:T(1,128)} %bitcast.7, f32[1,512]{1,0:T(1,128)} %bitcast.8, ...), custom_call_target="tpu_custom_call" | custom-call | tf_op jit(solution)/shard_map/pallas_call | solution.py:638
  63.4 1.1 %convert.1 = f32[4,256,256]{2,1,0:T(8,128)} convert(bf16[4,256,256]{2,1,0:T(8,128)(2,1)S(1)} %bitcast.5) | non-fusion elementwise | flops 262144 | bytes 1572864 | tf_op jit(solution)/shard_map/reshape | solution.py:704
  64.5 0.7 %copy.13 = bf16[8,16,1024]{2,1,0:T(8,128)(2,1)} copy(bf16[8,16,1024]{2,1,0:T(8,128)(2,1)S(1)} %get-tuple-element.8) | data formatting | bytes 524288

commit v4 on v3

--- a/solution.py
+++ b/solution.py
@@ -125,13 +125,12 @@
     mean = jnp.sum(ready * ready, axis=1, keepdims=True) * (1.0 / patch)
     normed_f = ready * lax.rsqrt(mean + 1e-05)
     normed = normed_f.astype(BF16)
-    work["normed_t"][...] = normed_f.T.astype(BF16)
+    work["normed"][...] = normed
     score_scale = (patch // HEADS) ** (-0.5)
     query = nn(normed, w_query_ref[...]).astype(BF16).astype(F32)
     work["query"][...] = (query * score_scale).astype(BF16)
     keys = nn(normed, w_key_ref[...]).astype(BF16)
     work["key"][...] = keys
-    work["key_t"][...] = keys.astype(F32).T.astype(BF16)
     values = nn(normed, w_value_ref[...]).astype(BF16)
     work["value"][...] = values
     work["value_t"][...] = values.astype(F32).T.astype(BF16)
@@ -213,6 +212,7 @@
 
 
 WORK = (
+    ("normed", 0, BF16),
     ("query", 0, BF16),
     ("key", 0, BF16),
     ("value", 0, BF16),
@@ -430,7 +430,7 @@
         ).start()
         return carry
 
-    early = members // 2
+    early = 1
     lax.fori_loop(1, members, send_ready, 0)
     lax.fori_loop(1, early, send_upstream, 0)
     own_upstream = pltpu.make_async_copy(
@@ -475,20 +475,8 @@
     tokens_copy.wait_recv()
     project_tokens(tokens_ref, hits_ref, columns_ref, weights, work)
     attend(columns_ref, work)
-    emit_attended(attended_ref, w_out_ref, work)
-
-    def give_back(step, carry):
-        peer = lax.rem(me + step, members)
-        remote(
-            rows_of(attended_ref, peer), block_of(returned_ref, me), 3, (slab, peer)
-        ).start()
-        return carry
-
-    lax.fori_loop(1, members, give_back, 0)
-    own_back = pltpu.make_async_copy(
-        rows_of(attended_ref, me), block_of(returned_ref, me), local_sem.at[2]
-    )
-    own_back.start()
+    for name in ("normed", "key"):
+        work[name + "_t"][...] = work[name][...].astype(F32).T.astype(BF16)
 
     def core_copy(part):
         return remote(core_out.at[part], core_in.at[part], 4 + 5 * part, core_peer)
@@ -582,8 +570,22 @@
         0, (nt(normed_t, work["grad_query_t"][...]), nn(normed_t, work["grad_key"][...]))
     )
     start_scatter(0)
+    emit_attended(attended_ref, w_out_ref, work)
     start_exchange(1)
     start_exchange(0)
+    def give_back(step, carry):
+        peer = lax.rem(me + step, members)
+        remote(
+            rows_of(attended_ref, peer), block_of(returned_ref, me), 3, (slab, peer)
+        ).start()
+        return carry
+
+    lax.fori_loop(1, members, give_back, 0)
+    own_back = pltpu.make_async_copy(
+        rows_of(attended_ref, me), block_of(returned_ref, me), local_sem.at[2]
+    )
+    own_back.start()
+
     start_gather(1)
     start_gather(0)
     start_last(1)
@@ -608,6 +610,20 @@
     for part in range(2):
         last_copy(part).wait_recv()
         own_summed(part).wait()
+
+
+def finish_kernel(returned_ref, summed_ref, out_ref, grads_ref, wide_ref, sems):
+    back = pltpu.make_async_copy(returned_ref, out_ref, sems.at[0])
+    back.start()
+    stores = []
+    for k in range(grads_ref.shape[0]):
+        part = summed_ref[k // CORES, k % CORES].astype(F32)
+        wide_ref[k] = part.reshape(wide_ref.shape[1:])
+        stores.append(pltpu.make_async_copy(wide_ref.at[k], grads_ref.at[k], sems.at[1 + k]))
+        stores[-1].start()
+    for store in stores:
+        store.wait()
+    back.wait()
 
 
 VMEM = pl.BlockSpec(memory_space=pltpu.VMEM)
@@ -701,7 +717,17 @@
             )
         )
     )
-    return (returned, summed.astype(F32).reshape(4, patch, patch))
+    return pl.pallas_call(
+        finish_kernel,
+        out_shape=(
+            jax.ShapeDtypeStruct(signal.shape, BF16),
+            jax.ShapeDtypeStruct((4, patch, patch), F32),
+        ),
+        in_specs=[VMEM, VMEM],
+        out_specs=(HBM, HBM),
+        scratch_shapes=[pltpu.VMEM((4, patch, patch), F32), pltpu.SemaphoreType.DMA((5,))],
+        compiler_params=pltpu.CompilerParams(vmem_limit_bytes=8 * 2**20),
+    )(returned, summed)
 
 
 def solution(mesh):

time: 65.3 us -> 64.9 us (level)
  Pallas kernels: 62.8 us -> 64.1 us
  other arithmetic: 1.06 us -> 0 us
  local copies, waits for them, and re-layouts: 0.7 us -> 0 us
    pallas_call x0 -> x1, Pallas kernels: none -> 1.09 us  [local(): pl.pallas_call(finish_kernel, out_shape=(jax.ShapeDtypeStruct(signal.shap...]
    reshape x1 -> x0, other arithmetic: 1.06 us -> none  [local(): return (returned, summed.astype(F32).reshape(4, patch, patch))]
    unnamed x1 -> x0, local copies, waits for them, and re-layouts: 0.7 us -> none
where the time goes in v4:
time: 64.9 us; the launch traced here: 64.7 us
  Pallas kernels  64.1 us (99%)
    pallas_call x1, Pallas kernels, local(): pl.pallas_call(functools.partial(step_kernel, slabs, members, (groups * t...  63 us

profile of v4, /device:TPU:1, one launch (start us, length us, event | category | flops | bytes accessed | tf_op | source)
XLA Modules:
  0.0 64.7 jit_solution(3303119370129240397)
XLA Ops:
  0.6 63.0 %shard_map.113 = (bf16[8,16,1024]{2,1,0:T(8,128)(2,1)S(1)}, bf16[2,2,32,8,256]{4,3,2,1,0:T(8,128)(2,1)S(1)}) custom-call(bf16[8,16,1024]{2,1,0:T(8,128)(2,1)} %signal_hbm.1, bf16[16,129]{1,0:T(8,128)(2,1)} %taps_hbm.1, s32[4,512]{1,0:T(4,128)} %bitcast.3, s32[1,512]{1,0:T(1,128)} %bitcast.4, f32[1,512]{1,0:T(1,128)} %bitcast.5, ...), custom_call_target="tpu_custom_call" | custom-call | tf_op jit(solution)/shard_map/pallas_call | solution.py:654
  63.7 1.1 %shard_map.114 = (bf16[8,16,1024]{2,1,0:T(8,128)(2,1)}, f32[4,256,256]{2,1,0:T(8,128)}) custom-call(bf16[8,16,1024]{2,1,0:T(8,128)(2,1)S(1)} %get-tuple-element.4.returned_ref, bf16[2,2,32,8,256]{4,3,2,1,0:T(8,128)(2,1)S(1)} %get-tuple-element.5.summed_ref), custom_call_target="tpu_custom_call" | custom-call | tf_op jit(solution)/shard_map/pallas_call | solution.py:720

commit v5 on v4

--- a/solution.py
+++ b/solution.py
@@ -154,9 +154,17 @@
 def attend(columns_ref, work):
     tokens, patch = work["key"].shape
     bias = wide(columns_ref[3], tokens)
+
+    def scores_of(h):
+        at, _ = head_slices(patch, h)
+        return nt(work["key"][:, at], one_of_pair(work["query"], h)) + bias
+
+    ahead = scores_of(0)
     for h in range(HEADS):
-        at, rows = head_slices(patch, h)
-        scores = nt(work["key"][:, at], one_of_pair(work["query"], h)) + bias
+        _, rows = head_slices(patch, h)
+        scores = ahead
+        if h + 1 < HEADS:
+            ahead = scores_of(h + 1)
         raised = jnp.exp(scores - jnp.max(scores, axis=0, keepdims=True))
         prob = raised * (1.0 / jnp.sum(raised, axis=0, keepdims=True))
         prob_low = prob.astype(BF16)

time: 64.9 us -> 64.8 us (level)
  no operation moved by 1% of the time
where the time goes in v5:
time: 64.8 us; the launch traced here: 64.7 us
  Pallas kernels  64.1 us (99%)
    pallas_call x1, Pallas kernels, local(): pl.pallas_call(functools.partial(step_kernel, slabs, members, (groups * t...  63 us

profile of v5, /device:TPU:1, one launch (start us, length us, event | category | flops | bytes accessed | tf_op | source)
XLA Modules:
  0.0 64.7 jit_solution(5401702717567758671)
XLA Ops:
  0.6 63.0 %shard_map.113 = (bf16[8,16,1024]{2,1,0:T(8,128)(2,1)S(1)}, bf16[2,2,32,8,256]{4,3,2,1,0:T(8,128)(2,1)S(1)}) custom-call(bf16[8,16,1024]{2,1,0:T(8,128)(2,1)} %signal_hbm.1, bf16[16,129]{1,0:T(8,128)(2,1)} %taps_hbm.1, s32[4,512]{1,0:T(4,128)} %bitcast.3, s32[1,512]{1,0:T(1,128)} %bitcast.4, f32[1,512]{1,0:T(1,128)} %bitcast.5, ...), custom_call_target="tpu_custom_call" | custom-call | tf_op jit(solution)/shard_map/pallas_call | solution.py:662
  63.6 1.1 %shard_map.114 = (bf16[8,16,1024]{2,1,0:T(8,128)(2,1)}, f32[4,256,256]{2,1,0:T(8,128)}) custom-call(bf16[8,16,1024]{2,1,0:T(8,128)(2,1)S(1)} %get-tuple-element.4.returned_ref, bf16[2,2,32,8,256]{4,3,2,1,0:T(8,128)(2,1)S(1)} %get-tuple-element.5.summed_ref), custom_call_target="tpu_custom_call" | custom-call | tf_op jit(solution)/shard_map/pallas_call | solution.py:728

commit v6 on v5

--- a/solution.py
+++ b/solution.py
@@ -438,7 +438,7 @@
         ).start()
         return carry
 
-    early = 1
+    early = members // 4
     lax.fori_loop(1, members, send_ready, 0)
     lax.fori_loop(1, early, send_upstream, 0)
     own_upstream = pltpu.make_async_copy(

time: 64.8 us -> 65.3 us (level)
  no operation moved by 1% of the time
where the time goes in v6:
time: 65.3 us; the launch traced here: 65.2 us
  Pallas kernels  64.5 us (99%)
    pallas_call x1, Pallas kernels, local(): pl.pallas_call(functools.partial(step_kernel, slabs, members, (groups * t...  63.4 us

profile of v6, /device:TPU:1, one launch (start us, length us, event | category | flops | bytes accessed | tf_op | source)
XLA Modules:
  0.0 65.2 jit_solution(6168570713122583345)
XLA Ops:
  0.6 63.4 %shard_map.113 = (bf16[8,16,1024]{2,1,0:T(8,128)(2,1)S(1)}, bf16[2,2,32,8,256]{4,3,2,1,0:T(8,128)(2,1)S(1)}) custom-call(bf16[8,16,1024]{2,1,0:T(8,128)(2,1)} %signal_hbm.1, bf16[16,129]{1,0:T(8,128)(2,1)} %taps_hbm.1, s32[4,512]{1,0:T(4,128)} %bitcast.3, s32[1,512]{1,0:T(1,128)} %bitcast.4, f32[1,512]{1,0:T(1,128)} %bitcast.5, ...), custom_call_target="tpu_custom_call" | custom-call | tf_op jit(solution)/shard_map/pallas_call | solution.py:662
  64.1 1.1 %shard_map.114 = (bf16[8,16,1024]{2,1,0:T(8,128)(2,1)}, f32[4,256,256]{2,1,0:T(8,128)}) custom-call(bf16[8,16,1024]{2,1,0:T(8,128)(2,1)S(1)} %get-tuple-element.4.returned_ref, bf16[2,2,32,8,256]{4,3,2,1,0:T(8,128)(2,1)S(1)} %get-tuple-element.5.summed_ref), custom_call_target="tpu_custom_call" | custom-call | tf_op jit(solution)/shard_map/pallas_call | solution.py:728
